TPU v7x, 32 devices: a whole 2x2x4 slice. The times are simulated.
32 devices in a mesh: elem: 16 (over z, x, core), band: 2 (over y).
Axes of the slice: x: 2, y: 2, z: 4, core: 2. Of those that a mesh axis runs over, the one named last changes fastest.
Arguments:
- basis: bfloat16 [256, 32, 16, 160], P('band', 'elem'), may hold values from -8 to 8
- hamiltonian: bfloat16 [32, 16, 7, 160, 160], P('elem'), may hold values from -0.09375 to 0.09375
- neighbours: int32 [32, 16, 6], P('elem'), may hold values from 0 to 511, as said below
Outputs:
- filtered: bfloat16 [256, 32, 16, 160], P('band', 'elem')
- intersection: float32 [256, 256], P('elem', 'band')
- projected: float32 [256, 256], P('elem', 'band')
Inputs may be any that keep to these rules, and one draw needn't show every extreme that they name: neighbours[z, s, d] = z2 * 16 + s2 names the element (z2, s2) that shares face d with element (z, s) on a periodic grid of 4 x 4 x 32 cells, whose cells are stored within each layer in an order of the draw; faces 0 to 3 lie in the same layer z, face 4 in layer z - 1 and face 5 in layer z + 1, both modulo 32.
All inputs are finite; a program needn't handle non-finite values.
Results may differ from a plain program's by a relative error of at most 0.0075.
Values may be sent and summed in bfloat16 or wider, within the bound.
A program may use at most 64 MiB of HBM per device.

v0:
```python
import jax
import jax.numpy as jnp
from jax import lax
from jax.sharding import PartitionSpec as P

DEGREE = 4


def extended_2(block, sides, width):
    for axis, dim in sides:
        count = lax.axis_size(axis)
        forward = [(i, i + 1) for i in range(count - 1)]
        forward.append((count - 1, 0))
        backward = [(target, source) for source, target in forward]
        low = lax.ppermute(
            lax.slice_in_dim(block, block.shape[dim] - width, None, axis=dim), axis, forward
        )
        high = lax.ppermute(lax.slice_in_dim(block, 0, width, axis=dim), axis, backward)
        block = jnp.concatenate([low, block, high], axis=dim)
    return block


def body(basis, hamiltonian, neighbours):
    width, layers, cells, functions = basis.shape
    elem_count = lax.axis_size("elem")
    depth = layers * elem_count
    first = lax.axis_index("elem") * layers
    layer_of = neighbours // cells
    relative = (layer_of - first + 1) % depth
    outer = relative * cells + neighbours % cells
    own = (jnp.arange(layers)[:, None] + 1) * cells + jnp.arange(cells)[None, :]
    table = jnp.concatenate([own[:, :, None], outer], axis=2)

    def apply_blocks(field):
        extended = extended_2(field, (("elem", 1),), 1)
        flat = extended.reshape(width, (layers + 2) * cells, functions)
        picked = jnp.take(flat, table, axis=1)
        return jnp.einsum(
            "zsdij,czsdj->czsi", hamiltonian, picked, preferred_element_type=jnp.float32
        )

    previous = basis
    current = apply_blocks(basis).astype(jnp.bfloat16)
    for step in range(DEGREE - 1):
        following = (2.0 * apply_blocks(current) - previous.astype(jnp.float32)).astype(
            jnp.bfloat16
        )
        previous, current = (current, following)
    image = apply_blocks(current).astype(jnp.bfloat16)
    factor = 1.0 / (depth * cells * functions)
    piece = lax.all_gather(current, "band", axis=0, tiled=True)
    left_part = jnp.einsum("kzsi,czsi->kc", piece, current, preferred_element_type=jnp.float32)
    right_part = jnp.einsum("kzsi,czsi->kc", piece, image, preferred_element_type=jnp.float32)
    partial_terms = jnp.stack([left_part, right_part])
    totals = lax.psum_scatter(partial_terms, "elem", scatter_dimension=1, tiled=True)
    return (current, totals[0] * factor, totals[1] * factor)


def solution(mesh):
    placed = (
        P("band", "elem", None, None),
        P("elem", None, None, None, None),
        P("elem", None, None),
    )
    return jax.shard_map(
        body,
        mesh=mesh,
        in_specs=placed,
        out_specs=(P("band", "elem", None, None), P("elem", "band"), P("elem", "band")),
        check_vma=False,
    )
```

profile of v0, /device:TPU:0, one launch (start us, length us, event | category | flops | bytes accessed | tf_op | source)
XLA Modules:
  0.0 281.0 jit_solution(16922853320731717165)
XLA Ops:
  7.2 1.4 fusion.80
  8.6 5.5 %collective-permute-start.1 = (bf16[128,1,16,160]{0,3,2,1:T(8,128)(2,1)S(1)}, bf16[128,1,16,160]{0,3,2,1:T(8,128)(2,1)S(1)}, u32[]{:S(2)}, u32[]{:S(2)}) collective-permute-start(bf16[128,1,16,160]{0,3,2,1:T(8,128)(2,1)S(1)} %get-tuple-element.15), channel_id=1, source_target_pairs={{2,0},{4,2},{6,4},{8,6},{10,8},{12,10},{14,12},{16,14},{18,16},{20... | collective-permute-start | bytes 1966088 | tf_op jit(solution)/shard_map/ppermute | solution.py:18
  14.6 7.6 %collective-permute-done.1 = bf16[128,1,16,160]{0,3,2,1:T(8,128)(2,1)S(1)} collective-permute-done((bf16[128,1,16,160]{0,3,2,1:T(8,128)(2,1)S(1)}, bf16[128,1,16,160]{0,3,2,1:T(8,128)(2,1)S(1)}, u32[]{:S(2)}, u32[]{:S(2)}) %collective-permute-start.1) | collective-permute-done | bytes 655392 | tf_op jit(solution)/shard_map/ppermute | solution.py:18
  22.2 4.8 %collective-permute-done = bf16[128,1,16,160]{0,3,2,1:T(8,128)(2,1)} collective-permute-done((bf16[128,1,16,160]{0,3,2,1:T(8,128)(2,1)S(1)}, bf16[128,1,16,160]{0,3,2,1:T(8,128)(2,1)}, u32[]{:S(2)}, u32[]{:S(2)}) %collective-permute-start) | collective-permute-done | bytes 655392 | tf_op jit(solution)/shard_map/ppermute | solution.py:15
  27.0 1.8 pad_maximum_fusion
  28.8 9.4 %gather_fusion = bf16[224,128,160]{1,2,0:T(8,128)(2,1)} fusion(bf16[128,64,160]{0,2,1:T(8,128)(2,1)S(1)} %bitcast.108, s32[1024]{0:T(1024)S(1)} %pad_clamp_fusion), kind=kCustom, calls=%fused_computation.clone | custom fusion | bytes 18350976 | tf_op jit(solution)/shard_map/jit(_take)/gather | solution.py:37
  38.2 11.3 %fusion.42 = bf16[128,2,16,160]{0,3,2,1:T(8,128)(2,1)S(1)} fusion(bf16[2,16,7,160,160]{4,3,2,1,0:T(8,128)(2,1)} %param.6, bf16[2,16,7,128,160]{3,4,2,1,0:T(8,128)(2,1)} %bitcast.114, pred[2,16,7]{2,1,0:T(8,128)(4,1)S(1)} %copy.14), kind=kOutput, calls=%fused_computation.49 | convolution fusion | flops 1473249280 | bytes 21954784 | tf_op jit(solution)/shard_map/zsdij,czsdj->czsi/dot_general | solution.py:38
  50.2 7.6 %collective-permute-done.3 = bf16[128,1,16,160]{0,3,2,1:T(8,128)(2,1)S(1)} collective-permute-done((bf16[128,1,16,160]{0,3,2,1:T(8,128)(2,1)S(1)}, bf16[128,1,16,160]{0,3,2,1:T(8,128)(2,1)S(1)}, u32[]{:S(2)}, u32[]{:S(2)}) %collective-permute-start.3) | collective-permute-done | bytes 655392 | tf_op jit(solution)/shard_map/ppermute | solution.py:18
  57.8 5.2 %collective-permute-done.2 = bf16[128,1,16,160]{0,3,2,1:T(8,128)(2,1)S(1)} collective-permute-done((bf16[128,1,16,160]{0,3,2,1:T(8,128)(2,1)S(1)}, bf16[128,1,16,160]{0,3,2,1:T(8,128)(2,1)S(1)}, u32[]{:S(2)}, u32[]{:S(2)}) %collective-permute-start.2) | collective-permute-done | bytes 655392 | tf_op jit(solution)/shard_map/ppermute | solution.py:15
  63.3 9.4 %gather_fusion.1 = bf16[224,128,160]{1,2,0:T(8,128)(2,1)} fusion(bf16[128,64,160]{0,2,1:T(8,128)(2,1)S(1)} %bitcast.109, s32[1024]{0:T(1024)S(1)} %pad_clamp_fusion), kind=kCustom, calls=%fused_computation.1.clone | custom fusion | bytes 18350976 | tf_op jit(solution)/shard_map/jit(_take)/gather | solution.py:37
  72.7 11.8 %fusion.25 = bf16[128,2,16,160]{0,3,2,1:T(8,128)(2,1)S(1)} fusion(bf16[128,2,16,160]{0,3,2,1:T(8,128)(2,1)} %param.5, bf16[2,16,7,160,160]{4,3,2,1,0:T(8,128)(2,1)} %param.6, bf16[2,16,7,128,160]{3,4,2,1,0:T(8,128)(2,1)} %bitcast.115, pred[2,16,7]{2,1,0:T(8,128)(4,1)S(1)} %copy.14), kind=kOutput, calls=%fused_computation.42 | convolution fusion | flops 1475215360 | bytes 23265504 | tf_op jit(solution)/shard_map/zsdij,czsdj->czsi/dot_general | solution.py:38
  84.7 4.0 %collective-permute-start.4 = (bf16[128,1,16,160]{0,3,2,1:T(8,128)(2,1)S(1)}, bf16[128,1,16,160]{0,3,2,1:T(8,128)(2,1)S(1)}, u32[]{:S(2)}, u32[]{:S(2)}) collective-permute-start(bf16[128,1,16,160]{0,3,2,1:T(8,128)(2,1)S(1)} %get-tuple-element.10), channel_id=1, source_target_pairs={{0,2},{2,4},{4,6},{6,8},{8,10},{10,12},{12,14},{14,16},{16,18},{18... | collective-permute-start | bytes 1966088 | tf_op jit(solution)/shard_map/ppermute | solution.py:15
  88.7 4.1 %collective-permute-done.5 = bf16[128,1,16,160]{0,3,2,1:T(8,128)(2,1)S(1)} collective-permute-done((bf16[128,1,16,160]{0,3,2,1:T(8,128)(2,1)S(1)}, bf16[128,1,16,160]{0,3,2,1:T(8,128)(2,1)S(1)}, u32[]{:S(2)}, u32[]{:S(2)}) %collective-permute-start.5) | collective-permute-done | bytes 655392 | tf_op jit(solution)/shard_map/ppermute | solution.py:18
  92.8 7.4 %collective-permute-done.4 = bf16[128,1,16,160]{0,3,2,1:T(8,128)(2,1)S(1)} collective-permute-done((bf16[128,1,16,160]{0,3,2,1:T(8,128)(2,1)S(1)}, bf16[128,1,16,160]{0,3,2,1:T(8,128)(2,1)S(1)}, u32[]{:S(2)}, u32[]{:S(2)}) %collective-permute-start.4) | collective-permute-done | bytes 655392 | tf_op jit(solution)/shard_map/ppermute | solution.py:15
  100.5 9.4 %gather_fusion.2 = bf16[224,128,160]{1,2,0:T(8,128)(2,1)} fusion(bf16[128,64,160]{0,2,1:T(8,128)(2,1)S(1)} %bitcast.110, s32[1024]{0:T(1024)S(1)} %pad_clamp_fusion), kind=kCustom, calls=%fused_computation.2.clone | custom fusion | bytes 18350976 | tf_op jit(solution)/shard_map/jit(_take)/gather | solution.py:37
  109.9 11.8 %fusion.24 = bf16[128,2,16,160]{0,3,2,1:T(8,128)(2,1)S(1)} fusion(bf16[128,2,16,160]{0,3,2,1:T(8,128)(2,1)} %copy-done.2, bf16[2,16,7,160,160]{4,3,2,1,0:T(8,128)(2,1)} %param.6, bf16[2,16,7,128,160]{3,4,2,1,0:T(8,128)(2,1)} %bitcast.112, pred[2,16,7]{2,1,0:T(8,128)(4,1)S(1)} %copy.14), kind=kOutput, calls=%fused_computation.39 | convolution fusion | flops 1475215360 | bytes 23265504 | tf_op jit(solution)/shard_map/zsdij,czsdj->czsi/dot_general | solution.py:38
  121.8 5.8 %collective-permute-start.6 = (bf16[128,1,16,160]{0,3,2,1:T(8,128)(2,1)S(1)}, bf16[128,1,16,160]{0,3,2,1:T(8,128)(2,1)S(1)}, u32[]{:S(2)}, u32[]{:S(2)}) collective-permute-start(bf16[128,1,16,160]{0,3,2,1:T(8,128)(2,1)S(1)} %get-tuple-element.8), channel_id=1, source_target_pairs={{0,2},{2,4},{4,6},{6,8},{8,10},{10,12},{12,14},{14,16},{16,18},{18... | collective-permute-start | bytes 1966088 | tf_op jit(solution)/shard_map/ppermute | solution.py:15
  127.6 2.3 collective-permute-done.7
  129.9 6.1 %collective-permute-done.6 = bf16[128,1,16,160]{0,3,2,1:T(8,128)(2,1)S(1)} collective-permute-done((bf16[128,1,16,160]{0,3,2,1:T(8,128)(2,1)S(1)}, bf16[128,1,16,160]{0,3,2,1:T(8,128)(2,1)S(1)}, u32[]{:S(2)}, u32[]{:S(2)}) %collective-permute-start.6) | collective-permute-done | bytes 655392 | tf_op jit(solution)/shard_map/ppermute | solution.py:15
  136.3 9.4 %gather_fusion.3 = bf16[224,128,160]{1,2,0:T(8,128)(2,1)} fusion(bf16[128,64,160]{0,2,1:T(8,128)(2,1)S(1)} %bitcast.106, s32[1024]{0:T(1024)S(1)} %pad_clamp_fusion), kind=kCustom, calls=%fused_computation.3.clone | custom fusion | bytes 18350976 | tf_op jit(solution)/shard_map/jit(_take)/gather | solution.py:37
  145.7 12.9 %fusion.23 = bf16[128,2,16,160]{0,3,2,1:T(8,128)(2,1)} fusion(bf16[128,2,16,160]{0,3,2,1:T(8,128)(2,1)} %copy-done.1, bf16[2,16,7,160,160]{4,3,2,1,0:T(8,128)(2,1)} %param.6, bf16[2,16,7,128,160]{3,4,2,1,0:T(8,128)(2,1)} %bitcast.113, pred[2,16,7]{2,1,0:T(8,128)(4,1)S(1)} %copy.14), kind=kOutput, calls=%fused_computation.36 | convolution fusion | flops 1475215360 | bytes 23265504 | tf_op jit(solution)/shard_map/zsdij,czsdj->czsi/dot_general | solution.py:38
  158.7 1.5 fusion.76
  160.2 6.8 %collective-permute-start.8 = (bf16[128,1,16,160]{0,3,2,1:T(8,128)(2,1)S(1)}, bf16[128,1,16,160]{0,3,2,1:T(8,128)(2,1)S(1)}, u32[]{:S(2)}, u32[]{:S(2)}) collective-permute-start(bf16[128,1,16,160]{0,3,2,1:T(8,128)(2,1)S(1)} %get-tuple-element.6), channel_id=1, source_target_pairs={{0,2},{2,4},{4,6},{6,8},{8,10},{10,12},{12,14},{14,16},{16,18},{18... | collective-permute-start | bytes 1966088 | tf_op jit(solution)/shard_map/ppermute | solution.py:15
  167.0 1.5 collective-permute-done.9
  168.6 6.5 %collective-permute-done.8 = bf16[128,1,16,160]{0,3,2,1:T(8,128)(2,1)S(1)} collective-permute-done((bf16[128,1,16,160]{0,3,2,1:T(8,128)(2,1)S(1)}, bf16[128,1,16,160]{0,3,2,1:T(8,128)(2,1)S(1)}, u32[]{:S(2)}, u32[]{:S(2)}) %collective-permute-start.8) | collective-permute-done | bytes 655392 | tf_op jit(solution)/shard_map/ppermute | solution.py:15
  175.4 9.4 %gather_fusion.4 = bf16[224,128,160]{1,2,0:T(8,128)(2,1)} fusion(bf16[128,64,160]{0,2,1:T(8,128)(2,1)S(1)} %bitcast.107, s32[1024]{0:T(1024)S(1)} %pad_clamp_fusion), kind=kCustom, calls=%fused_computation.4.clone | custom fusion | bytes 18350976 | tf_op jit(solution)/shard_map/jit(_take)/gather | solution.py:37
  184.8 17.0 %all-gather.2.cloned.1.call-done = bf16[256,2,16,160]{0,3,2,1:T(8,128)(2,1)} async-done(((bf16[128,2,16,160]{0,3,2,1:T(8,128)(2,1)}), bf16[256,2,16,160]{0,3,2,1:T(8,128)(2,1)}) %all-gather.2.cloned.1.call-update) | async-done | bytes 2621456 | tf_op jit(solution)/shard_map/all_gather | solution.py:51
  201.8 3.1 %fusion.55 = f32[1,256,128]{2,1,0:T(8,128)S(1)} fusion(bf16[128,2,16,160]{0,3,2,1:T(8,128)(2,1)} %fusion.23, bf16[256,2,16,160]{0,3,2,1:T(8,128)(2,1)} %all-gather.2.cloned.1.call-done), kind=kOutput, calls=%fused_computation.52 | convolution fusion | flops 335544320 | bytes 4063232 | tf_op jit(solution)/shard_map/kzsi,czsi->kc/dot_general | solution.py:52
  205.0 11.3 %fusion.60 = f32[1,256,128]{2,1,0:T(8,128)S(1)} fusion(bf16[2,16,7,160,160]{4,3,2,1,0:T(8,128)(2,1)} %param.6, bf16[256,2,16,160]{0,3,2,1:T(8,128)(2,1)S(1)} %copy-done.4, bf16[2,16,7,128,160]{3,4,2,1,0:T(8,128)(2,1)} %bitcast.111, pred[2,16,7]{2,1,0:T(8,128)(4,1)S(1)} %copy.14), kind=kOutput, calls=%fused_computation.53 | convolution fusion | flops 1808793600 | bytes 23396576 | tf_op jit(solution)/shard_map/kzsi,czsi->kc/dot_general | solution.py:53
  216.2 0.7 pad_maximum_fusion.5
  217.0 55.9 %reduce-scatter.2.cloned.1.call-done = f32[2,16,128]{2,1,0:T(8,128)} async-done(((f32[2,256,128]{2,1,0:T(8,128)}), f32[2,16,128]{2,1,0:T(8,128)}) %reduce-scatter.2.cloned.1.call-update) | async-done | bytes 16400 | tf_op jit(solution)/shard_map/reduce_scatter | solution.py:55
  272.9 1.3 fusion.67
  (35 shorter events, 2.8 us)
Async XLA Ops:
  7.2 7.0 %copy-start.3 = (s32[2,16,6]{1,0,2:T(2,128)S(1)}, s32[2,16,6]{1,0,2:T(2,128)}, u32[]{:S(2)}) copy-start(s32[2,16,6]{1,0,2:T(2,128)} %param.7) | copy-start | bytes 2308
  7.2 194.6 %all-gather.2.cloned.1.call-start = ((), (), s32[]{:S(2)}) async-start(), calls=%async_computation.1 | async-start | bytes 3932160 | tf_op jit(solution)/shard_map/all_gather | solution.py:51
  8.6 13.6 %collective-permute-start.1 = (bf16[128,1,16,160]{0,3,2,1:T(8,128)(2,1)S(1)}, bf16[128,1,16,160]{0,3,2,1:T(8,128)(2,1)S(1)}, u32[]{:S(2)}, u32[]{:S(2)}) collective-permute-start(bf16[128,1,16,160]{0,3,2,1:T(8,128)(2,1)S(1)} %get-tuple-element.15), channel_id=1, source_target_pairs={{2,0},{4,2},{6,4},{8,6},{10,8},{12,10},{14,12},{16,14},{18,16},{20... | collective-permute-start | bytes 1966088 | tf_op jit(solution)/shard_map/ppermute | solution.py:18
  14.1 12.9 %collective-permute-start = (bf16[128,1,16,160]{0,3,2,1:T(8,128)(2,1)S(1)}, bf16[128,1,16,160]{0,3,2,1:T(8,128)(2,1)}, u32[]{:S(2)}, u32[]{:S(2)}) collective-permute-start(bf16[128,1,16,160]{0,3,2,1:T(8,128)(2,1)S(1)} %get-tuple-element.14), channel_id=1, source_target_pairs={{0,2},{2,4},{4,6},{6,8},{8,10},{10,12},{12,14},{14,16},{16,18},{18... | collective-permute-start | bytes 1966088 | tf_op jit(solution)/shard_map/ppermute | solution.py:15
  49.5 13.8 %copy-start.2 = (bf16[128,2,16,160]{0,3,2,1:T(8,128)(2,1)}, bf16[128,2,16,160]{0,3,2,1:T(8,128)(2,1)S(1)}, u32[]{:S(2)}) copy-start(bf16[128,2,16,160]{0,3,2,1:T(8,128)(2,1)S(1)} %fusion.42) | copy-start | bytes 3932164
  49.6 8.2 %collective-permute-start.3 = (bf16[128,1,16,160]{0,3,2,1:T(8,128)(2,1)S(1)}, bf16[128,1,16,160]{0,3,2,1:T(8,128)(2,1)S(1)}, u32[]{:S(2)}, u32[]{:S(2)}) collective-permute-start(bf16[128,1,16,160]{0,3,2,1:T(8,128)(2,1)S(1)} %get-tuple-element.13), channel_id=1, source_target_pairs={{2,0},{4,2},{6,4},{8,6},{10,8},{12,10},{14,12},{16,14},{18,16},{20... | collective-permute-start | bytes 1966088 | tf_op jit(solution)/shard_map/ppermute | solution.py:18
  49.7 13.3 %collective-permute-start.2 = (bf16[128,1,16,160]{0,3,2,1:T(8,128)(2,1)S(1)}, bf16[128,1,16,160]{0,3,2,1:T(8,128)(2,1)S(1)}, u32[]{:S(2)}, u32[]{:S(2)}) collective-permute-start(bf16[128,1,16,160]{0,3,2,1:T(8,128)(2,1)S(1)} %get-tuple-element.12), channel_id=1, source_target_pairs={{0,2},{2,4},{4,6},{6,8},{8,10},{10,12},{12,14},{14,16},{16,18},{18... | collective-permute-start | bytes 1966088 | tf_op jit(solution)/shard_map/ppermute | solution.py:15
  84.5 15.9 %copy-start.1 = (bf16[128,2,16,160]{0,3,2,1:T(8,128)(2,1)}, bf16[128,2,16,160]{0,3,2,1:T(8,128)(2,1)S(1)}, u32[]{:S(2)}) copy-start(bf16[128,2,16,160]{0,3,2,1:T(8,128)(2,1)S(1)} %fusion.25) | copy-start | bytes 3932164
  84.6 8.2 %collective-permute-start.5 = (bf16[128,1,16,160]{0,3,2,1:T(8,128)(2,1)S(1)}, bf16[128,1,16,160]{0,3,2,1:T(8,128)(2,1)S(1)}, u32[]{:S(2)}, u32[]{:S(2)}) collective-permute-start(bf16[128,1,16,160]{0,3,2,1:T(8,128)(2,1)S(1)} %get-tuple-element.11), channel_id=1, source_target_pairs={{2,0},{4,2},{6,4},{8,6},{10,8},{12,10},{14,12},{16,14},{18,16},{20... | collective-permute-start | bytes 1966088 | tf_op jit(solution)/shard_map/ppermute | solution.py:18
  84.7 15.4 %collective-permute-start.4 = (bf16[128,1,16,160]{0,3,2,1:T(8,128)(2,1)S(1)}, bf16[128,1,16,160]{0,3,2,1:T(8,128)(2,1)S(1)}, u32[]{:S(2)}, u32[]{:S(2)}) collective-permute-start(bf16[128,1,16,160]{0,3,2,1:T(8,128)(2,1)S(1)} %get-tuple-element.10), channel_id=1, source_target_pairs={{0,2},{2,4},{4,6},{6,8},{8,10},{10,12},{12,14},{14,16},{16,18},{18... | collective-permute-start | bytes 1966088 | tf_op jit(solution)/shard_map/ppermute | solution.py:15
  121.8 8.2 %collective-permute-start.7 = (bf16[128,1,16,160]{0,3,2,1:T(8,128)(2,1)S(1)}, bf16[128,1,16,160]{0,3,2,1:T(8,128)(2,1)S(1)}, u32[]{:S(2)}, u32[]{:S(2)}) collective-permute-start(bf16[128,1,16,160]{0,3,2,1:T(8,128)(2,1)S(1)} %get-tuple-element.9), channel_id=1, source_target_pairs={{2,0},{4,2},{6,4},{8,6},{10,8},{12,10},{14,12},{16,14},{18,16},{20... | collective-permute-start | bytes 1966088 | tf_op jit(solution)/shard_map/ppermute | solution.py:18
  121.8 14.2 %collective-permute-start.6 = (bf16[128,1,16,160]{0,3,2,1:T(8,128)(2,1)S(1)}, bf16[128,1,16,160]{0,3,2,1:T(8,128)(2,1)S(1)}, u32[]{:S(2)}, u32[]{:S(2)}) collective-permute-start(bf16[128,1,16,160]{0,3,2,1:T(8,128)(2,1)S(1)} %get-tuple-element.8), channel_id=1, source_target_pairs={{0,2},{2,4},{4,6},{6,8},{8,10},{10,12},{12,14},{14,16},{16,18},{18... | collective-permute-start | bytes 1966088 | tf_op jit(solution)/shard_map/ppermute | solution.py:15
  158.6 114.3 %reduce-scatter.2.cloned.1.call-start = ((), (), s32[]{:S(2)}) async-start(), calls=%async_computation.2 | async-start | bytes 278528 | tf_op jit(solution)/shard_map/reduce_scatter | solution.py:55
  158.7 16.4 %copy-start = (bf16[128,2,16,160]{0,3,2,1:T(8,128)(2,1)S(1)}, bf16[128,2,16,160]{0,3,2,1:T(8,128)(2,1)}, u32[]{:S(2)}) copy-start(bf16[128,2,16,160]{0,3,2,1:T(8,128)(2,1)} %fusion.23) | copy-start | bytes 3932164
  160.2 8.4 %collective-permute-start.9 = (bf16[128,1,16,160]{0,3,2,1:T(8,128)(2,1)S(1)}, bf16[128,1,16,160]{0,3,2,1:T(8,128)(2,1)S(1)}, u32[]{:S(2)}, u32[]{:S(2)}) collective-permute-start(bf16[128,1,16,160]{0,3,2,1:T(8,128)(2,1)S(1)} %get-tuple-element.7), channel_id=1, source_target_pairs={{2,0},{4,2},{6,4},{8,6},{10,8},{12,10},{14,12},{16,14},{18,16},{20... | collective-permute-start | bytes 1966088 | tf_op jit(solution)/shard_map/ppermute | solution.py:18
  160.2 14.9 %collective-permute-start.8 = (bf16[128,1,16,160]{0,3,2,1:T(8,128)(2,1)S(1)}, bf16[128,1,16,160]{0,3,2,1:T(8,128)(2,1)S(1)}, u32[]{:S(2)}, u32[]{:S(2)}) collective-permute-start(bf16[128,1,16,160]{0,3,2,1:T(8,128)(2,1)S(1)} %get-tuple-element.6), channel_id=1, source_target_pairs={{0,2},{2,4},{4,6},{6,8},{8,10},{10,12},{12,14},{14,16},{16,18},{18... | collective-permute-start | bytes 1966088 | tf_op jit(solution)/shard_map/ppermute | solution.py:15
  201.8 3.1 %copy-start.4 = (bf16[256,2,16,160]{0,3,2,1:T(8,128)(2,1)S(1)}, bf16[256,2,16,160]{0,3,2,1:T(8,128)(2,1)}, u32[]{:S(2)}) copy-start(bf16[256,2,16,160]{0,3,2,1:T(8,128)(2,1)} %all-gather.2.cloned.1.call-done) | copy-start | bytes 7864324
Sparse Core Ops, SparseCore 0:
  158.7 43.0 all-gather.1
  217.1 55.7 reduce-scatter.1
where the time goes:
time: 281 us
  waiting for transfers between devices  126 us (45%)
  matrix products  62.2 us (22%)
  local copies, waits for them, and re-layouts  50.3 us (18%)
  starting transfers between devices  22.8 us (8%)
  between operations  14.2 us (5%)
  other arithmetic  5.15 us (2%)
    reduce_scatter x1, waiting for transfers between devices, body(): lax.psum_scatter(partial_terms, 'elem', scatter_dimension=1, tiled=True)  55.9 us
    dot_general x4, matrix products, apply_blocks(): jnp.einsum('zsdij,czsdj->czsi', hamiltonian, picked, preferred_element_ty...  47.8 us
    gather x5, local copies, waits for them, and re-layouts, apply_blocks(): picked = jnp.take(flat, table, axis=1)  46.9 us
    ppermute x5, waiting for transfers between devices, extended_2(): lax.ppermute(lax.slice_in_dim(block, block.shape[dim] - width, None, axis...  30 us
    ppermute x5, waiting for transfers between devices, extended_2(): lax.ppermute(lax.slice_in_dim(block, 0, width, axis=dim), axis, backward)  23.2 us
    ppermute x5, starting transfers between devices, extended_2(): lax.ppermute(lax.slice_in_dim(block, block.shape[dim] - width, None, axis...  17 us
    all_gather x1, waiting for transfers between devices, body(): piece = lax.all_gather(current, 'band', axis=0, tiled=True)  17 us
    dot_general x1, matrix products, body(): jnp.einsum('kzsi,czsi->kc', piece, image, preferred_element_type=jnp.floa...  11.3 us
  transfers between devices with their start and end apart: 12, of which 12 were waited for; matrix products, arithmetic and copies ran while one was open for 4% of the time, Pallas kernels for 0%

commit v1 on v0

--- a/solution.py
+++ b/solution.py
@@ -4,6 +4,18 @@
 from jax.sharding import PartitionSpec as P
 
 DEGREE = 4
+
+
+def gather_by_bits(array, axis, dim):
+    ways, here, step = (lax.axis_size(axis), lax.axis_index(axis), array.shape[dim])
+    line, have = (array, 1)
+    while have < ways:
+        line = jnp.concatenate(
+            [line, lax.ppermute(line, axis, [(d, (d - have) % ways) for d in range(ways)])],
+            axis=dim,
+        )
+        have = 2 * have
+    return jnp.roll(line, here * step, axis=dim)
 
 
 def extended_2(block, sides, width):
@@ -48,7 +60,7 @@
         previous, current = (current, following)
     image = apply_blocks(current).astype(jnp.bfloat16)
     factor = 1.0 / (depth * cells * functions)
-    piece = lax.all_gather(current, "band", axis=0, tiled=True)
+    piece = gather_by_bits(current, "band", 0)
     left_part = jnp.einsum("kzsi,czsi->kc", piece, current, preferred_element_type=jnp.float32)
     right_part = jnp.einsum("kzsi,czsi->kc", piece, image, preferred_element_type=jnp.float32)
     partial_terms = jnp.stack([left_part, right_part])

time: 281 us -> 274 us (0.975)
  waiting for transfers between devices: 126 us -> 113 us
  other arithmetic: 5.15 us -> 10.7 us
    all_gather x1 -> x0, waiting for transfers between devices: 17 us -> none  [body(): piece = lax.all_gather(current, 'band', axis=0, tiled=True)]
    reduce_scatter x1, waiting for transfers between devices: 55.9 us -> 60 us  [body(): lax.psum_scatter(partial_terms, 'elem', scatter_dimension=1, tiled=True)]
    concatenate x0 -> x1, other arithmetic: none -> 4.06 us  [gather_by_bits(): return jnp.roll(line, here * step, axis=dim)]
  transfers between devices with their start and end apart: 12 -> 12, of which waited for: 12 -> 11; matrix products, arithmetic and copies ran while one was open for 4% -> 5% of each run, Pallas kernels for 0% -> 0%
where the time goes in v1:
time: 274 us
  waiting for transfers between devices  113 us (41%)
  matrix products  61.3 us (22%)
  local copies, waits for them, and re-layouts  50.1 us (18%)
  starting transfers between devices  24.3 us (9%)
  between operations  14.2 us (5%)
  other arithmetic  10.7 us (4%)
    reduce_scatter x1, waiting for transfers between devices, body(): lax.psum_scatter(partial_terms, 'elem', scatter_dimension=1, tiled=True)  60 us
    dot_general x4, matrix products, apply_blocks(): jnp.einsum('zsdij,czsdj->czsi', hamiltonian, picked, preferred_element_ty...  47.8 us
    gather x5, local copies, waits for them, and re-layouts, apply_blocks(): picked = jnp.take(flat, table, axis=1)  46.8 us
    ppermute x5, waiting for transfers between devices, extended_2(): lax.ppermute(lax.slice_in_dim(block, block.shape[dim] - width, None, axis...  30.4 us
    ppermute x5, waiting for transfers between devices, extended_2(): lax.ppermute(lax.slice_in_dim(block, 0, width, axis=dim), axis, backward)  23 us
    ppermute x5, starting transfers between devices, extended_2(): lax.ppermute(lax.slice_in_dim(block, block.shape[dim] - width, None, axis...  17 us
    dot_general x1, matrix products, body(): jnp.einsum('kzsi,czsi->kc', piece, image, preferred_element_type=jnp.floa...  11.3 us
    ppermute x5, starting transfers between devices, extended_2(): lax.ppermute(lax.slice_in_dim(block, 0, width, axis=dim), axis, backward)  5.73 us
  transfers between devices with their start and end apart: 12, of which 11 were waited for; matrix products, arithmetic and copies ran while one was open for 5% of the time, Pallas kernels for 0%

profile of v1, /device:TPU:0, one launch (start us, length us, event | category | flops | bytes accessed | tf_op | source)
XLA Modules:
  0.0 274.1 jit_solution(14032619705640276675)
XLA Ops:
  7.2 1.4 fusion.83
  8.6 5.5 %collective-permute-start.1 = (bf16[128,1,16,160]{0,3,2,1:T(8,128)(2,1)S(1)}, bf16[128,1,16,160]{0,3,2,1:T(8,128)(2,1)S(1)}, u32[]{:S(2)}, u32[]{:S(2)}) collective-permute-start(bf16[128,1,16,160]{0,3,2,1:T(8,128)(2,1)S(1)} %get-tuple-element.15), channel_id=1, source_target_pairs={{2,0},{4,2},{6,4},{8,6},{10,8},{12,10},{14,12},{16,14},{18,16},{20... | collective-permute-start | bytes 1966088 | tf_op jit(solution)/shard_map/ppermute | solution.py:30
  14.6 7.6 %collective-permute-done.1 = bf16[128,1,16,160]{0,3,2,1:T(8,128)(2,1)S(1)} collective-permute-done((bf16[128,1,16,160]{0,3,2,1:T(8,128)(2,1)S(1)}, bf16[128,1,16,160]{0,3,2,1:T(8,128)(2,1)S(1)}, u32[]{:S(2)}, u32[]{:S(2)}) %collective-permute-start.1) | collective-permute-done | bytes 655392 | tf_op jit(solution)/shard_map/ppermute | solution.py:30
  22.2 4.8 %collective-permute-done = bf16[128,1,16,160]{0,3,2,1:T(8,128)(2,1)} collective-permute-done((bf16[128,1,16,160]{0,3,2,1:T(8,128)(2,1)S(1)}, bf16[128,1,16,160]{0,3,2,1:T(8,128)(2,1)}, u32[]{:S(2)}, u32[]{:S(2)}) %collective-permute-start) | collective-permute-done | bytes 655392 | tf_op jit(solution)/shard_map/ppermute | solution.py:27
  27.0 1.8 pad_maximum_fusion
  28.8 9.4 %gather_fusion = bf16[224,128,160]{1,2,0:T(8,128)(2,1)} fusion(bf16[128,64,160]{0,2,1:T(8,128)(2,1)S(1)} %bitcast.108, s32[1024]{0:T(1024)S(1)} %pad_clamp_fusion), kind=kCustom, calls=%fused_computation.clone | custom fusion | bytes 18350976 | tf_op jit(solution)/shard_map/jit(_take)/gather | solution.py:49
  38.2 11.3 %fusion.45 = bf16[128,2,16,160]{0,3,2,1:T(8,128)(2,1)S(1)} fusion(bf16[2,16,7,160,160]{4,3,2,1,0:T(8,128)(2,1)} %param.6, bf16[2,16,7,128,160]{3,4,2,1,0:T(8,128)(2,1)} %bitcast.114, pred[2,16,7]{2,1,0:T(8,128)(4,1)S(1)} %copy.14), kind=kOutput, calls=%fused_computation.56 | convolution fusion | flops 1473249280 | bytes 21954784 | tf_op jit(solution)/shard_map/zsdij,czsdj->czsi/dot_general | solution.py:50
  50.2 7.6 %collective-permute-done.3 = bf16[128,1,16,160]{0,3,2,1:T(8,128)(2,1)S(1)} collective-permute-done((bf16[128,1,16,160]{0,3,2,1:T(8,128)(2,1)S(1)}, bf16[128,1,16,160]{0,3,2,1:T(8,128)(2,1)S(1)}, u32[]{:S(2)}, u32[]{:S(2)}) %collective-permute-start.3) | collective-permute-done | bytes 655392 | tf_op jit(solution)/shard_map/ppermute | solution.py:30
  57.8 5.2 %collective-permute-done.2 = bf16[128,1,16,160]{0,3,2,1:T(8,128)(2,1)S(1)} collective-permute-done((bf16[128,1,16,160]{0,3,2,1:T(8,128)(2,1)S(1)}, bf16[128,1,16,160]{0,3,2,1:T(8,128)(2,1)S(1)}, u32[]{:S(2)}, u32[]{:S(2)}) %collective-permute-start.2) | collective-permute-done | bytes 655392 | tf_op jit(solution)/shard_map/ppermute | solution.py:27
  63.3 9.4 %gather_fusion.1 = bf16[224,128,160]{1,2,0:T(8,128)(2,1)} fusion(bf16[128,64,160]{0,2,1:T(8,128)(2,1)S(1)} %bitcast.109, s32[1024]{0:T(1024)S(1)} %pad_clamp_fusion), kind=kCustom, calls=%fused_computation.1.clone | custom fusion | bytes 18350976 | tf_op jit(solution)/shard_map/jit(_take)/gather | solution.py:49
  72.7 11.8 %fusion.28 = bf16[128,2,16,160]{0,3,2,1:T(8,128)(2,1)S(1)} fusion(bf16[128,2,16,160]{0,3,2,1:T(8,128)(2,1)} %param.5, bf16[2,16,7,160,160]{4,3,2,1,0:T(8,128)(2,1)} %param.6, bf16[2,16,7,128,160]{3,4,2,1,0:T(8,128)(2,1)} %bitcast.115, pred[2,16,7]{2,1,0:T(8,128)(4,1)S(1)} %copy.14), kind=kOutput, calls=%fused_computation.49 | convolution fusion | flops 1475215360 | bytes 23265504 | tf_op jit(solution)/shard_map/zsdij,czsdj->czsi/dot_general | solution.py:50
  84.7 4.0 %collective-permute-start.4 = (bf16[128,1,16,160]{0,3,2,1:T(8,128)(2,1)S(1)}, bf16[128,1,16,160]{0,3,2,1:T(8,128)(2,1)S(1)}, u32[]{:S(2)}, u32[]{:S(2)}) collective-permute-start(bf16[128,1,16,160]{0,3,2,1:T(8,128)(2,1)S(1)} %get-tuple-element.10), channel_id=1, source_target_pairs={{0,2},{2,4},{4,6},{6,8},{8,10},{10,12},{12,14},{14,16},{16,18},{18... | collective-permute-start | bytes 1966088 | tf_op jit(solution)/shard_map/ppermute | solution.py:27
  88.6 4.1 %collective-permute-done.5 = bf16[128,1,16,160]{0,3,2,1:T(8,128)(2,1)S(1)} collective-permute-done((bf16[128,1,16,160]{0,3,2,1:T(8,128)(2,1)S(1)}, bf16[128,1,16,160]{0,3,2,1:T(8,128)(2,1)S(1)}, u32[]{:S(2)}, u32[]{:S(2)}) %collective-permute-start.5) | collective-permute-done | bytes 655392 | tf_op jit(solution)/shard_map/ppermute | solution.py:30
  92.8 7.4 %collective-permute-done.4 = bf16[128,1,16,160]{0,3,2,1:T(8,128)(2,1)S(1)} collective-permute-done((bf16[128,1,16,160]{0,3,2,1:T(8,128)(2,1)S(1)}, bf16[128,1,16,160]{0,3,2,1:T(8,128)(2,1)S(1)}, u32[]{:S(2)}, u32[]{:S(2)}) %collective-permute-start.4) | collective-permute-done | bytes 655392 | tf_op jit(solution)/shard_map/ppermute | solution.py:27
  100.4 9.4 %gather_fusion.2 = bf16[224,128,160]{1,2,0:T(8,128)(2,1)} fusion(bf16[128,64,160]{0,2,1:T(8,128)(2,1)S(1)} %bitcast.110, s32[1024]{0:T(1024)S(1)} %pad_clamp_fusion), kind=kCustom, calls=%fused_computation.2.clone | custom fusion | bytes 18350976 | tf_op jit(solution)/shard_map/jit(_take)/gather | solution.py:49
  109.8 11.8 %fusion.27 = bf16[128,2,16,160]{0,3,2,1:T(8,128)(2,1)S(1)} fusion(bf16[128,2,16,160]{0,3,2,1:T(8,128)(2,1)} %copy-done.1, bf16[2,16,7,160,160]{4,3,2,1,0:T(8,128)(2,1)} %param.6, bf16[2,16,7,128,160]{3,4,2,1,0:T(8,128)(2,1)} %bitcast.112, pred[2,16,7]{2,1,0:T(8,128)(4,1)S(1)} %copy.14), kind=kOutput, calls=%fused_computation.46 | convolution fusion | flops 1475215360 | bytes 23265504 | tf_op jit(solution)/shard_map/zsdij,czsdj->czsi/dot_general | solution.py:50
  121.8 5.8 %collective-permute-start.6 = (bf16[128,1,16,160]{0,3,2,1:T(8,128)(2,1)S(1)}, bf16[128,1,16,160]{0,3,2,1:T(8,128)(2,1)S(1)}, u32[]{:S(2)}, u32[]{:S(2)}) collective-permute-start(bf16[128,1,16,160]{0,3,2,1:T(8,128)(2,1)S(1)} %get-tuple-element.8), channel_id=1, source_target_pairs={{0,2},{2,4},{4,6},{6,8},{8,10},{10,12},{12,14},{14,16},{16,18},{18... | collective-permute-start | bytes 1966088 | tf_op jit(solution)/shard_map/ppermute | solution.py:27
  127.6 2.3 collective-permute-done.7
  129.9 6.1 %collective-permute-done.6 = bf16[128,1,16,160]{0,3,2,1:T(8,128)(2,1)S(1)} collective-permute-done((bf16[128,1,16,160]{0,3,2,1:T(8,128)(2,1)S(1)}, bf16[128,1,16,160]{0,3,2,1:T(8,128)(2,1)S(1)}, u32[]{:S(2)}, u32[]{:S(2)}) %collective-permute-start.6) | collective-permute-done | bytes 655392 | tf_op jit(solution)/shard_map/ppermute | solution.py:27
  136.3 9.4 %gather_fusion.3 = bf16[224,128,160]{1,2,0:T(8,128)(2,1)} fusion(bf16[128,64,160]{0,2,1:T(8,128)(2,1)S(1)} %bitcast.106, s32[1024]{0:T(1024)S(1)} %pad_clamp_fusion), kind=kCustom, calls=%fused_computation.3.clone | custom fusion | bytes 18350976 | tf_op jit(solution)/shard_map/jit(_take)/gather | solution.py:49
  145.7 12.9 %fusion.26 = bf16[128,2,16,160]{0,3,2,1:T(8,128)(2,1)} fusion(bf16[128,2,16,160]{0,3,2,1:T(8,128)(2,1)} %copy-done, bf16[2,16,7,160,160]{4,3,2,1,0:T(8,128)(2,1)} %param.6, bf16[2,16,7,128,160]{3,4,2,1,0:T(8,128)(2,1)} %bitcast.113, pred[2,16,7]{2,1,0:T(8,128)(4,1)S(1)} %copy.14), kind=kOutput, calls=%fused_computation.43 | convolution fusion | flops 1475215360 | bytes 23265504 | tf_op jit(solution)/shard_map/zsdij,czsdj->czsi/dot_general | solution.py:50
  158.5 1.5 collective-permute-start.8
  160.1 1.4 fusion.79
  161.5 6.8 %collective-permute-start.9 = (bf16[128,1,16,160]{0,3,2,1:T(8,128)(2,1)S(1)}, bf16[128,1,16,160]{0,3,2,1:T(8,128)(2,1)}, u32[]{:S(2)}, u32[]{:S(2)}) collective-permute-start(bf16[128,1,16,160]{0,3,2,1:T(8,128)(2,1)S(1)} %get-tuple-element.6), channel_id=1, source_target_pairs={{0,2},{2,4},{4,6},{6,8},{8,10},{10,12},{12,14},{14,16},{16,18},{18... | collective-permute-start | bytes 1966088 | tf_op jit(solution)/shard_map/ppermute | solution.py:27
  169.6 6.9 %collective-permute-done.9 = bf16[128,1,16,160]{0,3,2,1:T(8,128)(2,1)} collective-permute-done((bf16[128,1,16,160]{0,3,2,1:T(8,128)(2,1)S(1)}, bf16[128,1,16,160]{0,3,2,1:T(8,128)(2,1)}, u32[]{:S(2)}, u32[]{:S(2)}) %collective-permute-start.9) | collective-permute-done | bytes 655392 | tf_op jit(solution)/shard_map/ppermute | solution.py:27
  176.5 1.8 pad_maximum_fusion.4
  178.2 9.4 %gather_fusion.4 = bf16[224,128,160]{1,2,0:T(8,128)(2,1)} fusion(bf16[128,64,160]{0,2,1:T(8,128)(2,1)S(1)} %bitcast.107, s32[1024]{0:T(1024)S(1)} %pad_clamp_fusion), kind=kCustom, calls=%fused_computation.4.clone | custom fusion | bytes 18350976 | tf_op jit(solution)/shard_map/jit(_take)/gather | solution.py:49
  187.6 4.1 %fusion.25 = bf16[256,2,16,160]{0,3,2,1:T(8,128)(2,1)S(1)} fusion(s32[]{:T(128)S(6)} %select_n.39, bf16[128,2,16,160]{0,3,2,1:T(8,128)(2,1)} %fusion.26, bf16[128,2,16,160]{0,3,2,1:T(8,128)(2,1)} %collective-permute-done.8), kind=kLoop, calls=%fused_computation.35 | loop fusion | flops 10485760 | bytes 5242884 | tf_op jit(solution)/shard_map/jit(_roll_dynamic)/concatenate | solution.py:18
  191.7 2.2 fusion.58
  193.9 11.3 %fusion.63 = f32[1,256,128]{2,1,0:T(8,128)S(1)} fusion(bf16[2,16,7,160,160]{4,3,2,1,0:T(8,128)(2,1)} %param.6, bf16[256,2,16,160]{0,3,2,1:T(8,128)(2,1)S(1)} %fusion.25, bf16[2,16,7,128,160]{3,4,2,1,0:T(8,128)(2,1)} %bitcast.111, pred[2,16,7]{2,1,0:T(8,128)(4,1)S(1)} %copy.14), kind=kOutput, calls=%fused_computation.60 | convolution fusion | flops 1808793600 | bytes 23396576 | tf_op jit(solution)/shard_map/kzsi,czsi->kc/dot_general | solution.py:65
  205.9 60.0 %reduce-scatter.2.cloned.1.call-done = f32[2,16,128]{2,1,0:T(8,128)} async-done(((f32[2,256,128]{2,1,0:T(8,128)}), f32[2,16,128]{2,1,0:T(8,128)}) %reduce-scatter.2.cloned.1.call-update) | async-done | bytes 16400 | tf_op jit(solution)/shard_map/reduce_scatter | solution.py:67
  265.9 1.3 fusion.70
  (31 shorter events, 4.4 us)
Async XLA Ops:
  7.2 7.0 %copy-start.2 = (s32[2,16,6]{1,0,2:T(2,128)S(1)}, s32[2,16,6]{1,0,2:T(2,128)}, u32[]{:S(2)}) copy-start(s32[2,16,6]{1,0,2:T(2,128)} %param.7) | copy-start | bytes 2308
  7.2 258.7 %reduce-scatter.2.cloned.1.call-start = ((), (), s32[]{:S(2)}) async-start(), calls=%async_computation.1 | async-start | bytes 278528 | tf_op jit(solution)/shard_map/reduce_scatter | solution.py:67
  8.6 13.6 %collective-permute-start.1 = (bf16[128,1,16,160]{0,3,2,1:T(8,128)(2,1)S(1)}, bf16[128,1,16,160]{0,3,2,1:T(8,128)(2,1)S(1)}, u32[]{:S(2)}, u32[]{:S(2)}) collective-permute-start(bf16[128,1,16,160]{0,3,2,1:T(8,128)(2,1)S(1)} %get-tuple-element.15), channel_id=1, source_target_pairs={{2,0},{4,2},{6,4},{8,6},{10,8},{12,10},{14,12},{16,14},{18,16},{20... | collective-permute-start | bytes 1966088 | tf_op jit(solution)/shard_map/ppermute | solution.py:30
  14.1 12.9 %collective-permute-start = (bf16[128,1,16,160]{0,3,2,1:T(8,128)(2,1)S(1)}, bf16[128,1,16,160]{0,3,2,1:T(8,128)(2,1)}, u32[]{:S(2)}, u32[]{:S(2)}) collective-permute-start(bf16[128,1,16,160]{0,3,2,1:T(8,128)(2,1)S(1)} %get-tuple-element.14), channel_id=1, source_target_pairs={{0,2},{2,4},{4,6},{6,8},{8,10},{10,12},{12,14},{14,16},{16,18},{18... | collective-permute-start | bytes 1966088 | tf_op jit(solution)/shard_map/ppermute | solution.py:27
  49.5 13.8 %copy-start.1 = (bf16[128,2,16,160]{0,3,2,1:T(8,128)(2,1)}, bf16[128,2,16,160]{0,3,2,1:T(8,128)(2,1)S(1)}, u32[]{:S(2)}) copy-start(bf16[128,2,16,160]{0,3,2,1:T(8,128)(2,1)S(1)} %fusion.45) | copy-start | bytes 3932164
  49.6 8.2 %collective-permute-start.3 = (bf16[128,1,16,160]{0,3,2,1:T(8,128)(2,1)S(1)}, bf16[128,1,16,160]{0,3,2,1:T(8,128)(2,1)S(1)}, u32[]{:S(2)}, u32[]{:S(2)}) collective-permute-start(bf16[128,1,16,160]{0,3,2,1:T(8,128)(2,1)S(1)} %get-tuple-element.13), channel_id=1, source_target_pairs={{2,0},{4,2},{6,4},{8,6},{10,8},{12,10},{14,12},{16,14},{18,16},{20... | collective-permute-start | bytes 1966088 | tf_op jit(solution)/shard_map/ppermute | solution.py:30
  49.7 13.3 %collective-permute-start.2 = (bf16[128,1,16,160]{0,3,2,1:T(8,128)(2,1)S(1)}, bf16[128,1,16,160]{0,3,2,1:T(8,128)(2,1)S(1)}, u32[]{:S(2)}, u32[]{:S(2)}) collective-permute-start(bf16[128,1,16,160]{0,3,2,1:T(8,128)(2,1)S(1)} %get-tuple-element.12), channel_id=1, source_target_pairs={{0,2},{2,4},{4,6},{6,8},{8,10},{10,12},{12,14},{14,16},{16,18},{18... | collective-permute-start | bytes 1966088 | tf_op jit(solution)/shard_map/ppermute | solution.py:27
  84.5 15.9 %copy-start = (bf16[128,2,16,160]{0,3,2,1:T(8,128)(2,1)}, bf16[128,2,16,160]{0,3,2,1:T(8,128)(2,1)S(1)}, u32[]{:S(2)}) copy-start(bf16[128,2,16,160]{0,3,2,1:T(8,128)(2,1)S(1)} %fusion.28) | copy-start | bytes 3932164
  84.6 8.2 %collective-permute-start.5 = (bf16[128,1,16,160]{0,3,2,1:T(8,128)(2,1)S(1)}, bf16[128,1,16,160]{0,3,2,1:T(8,128)(2,1)S(1)}, u32[]{:S(2)}, u32[]{:S(2)}) collective-permute-start(bf16[128,1,16,160]{0,3,2,1:T(8,128)(2,1)S(1)} %get-tuple-element.11), channel_id=1, source_target_pairs={{2,0},{4,2},{6,4},{8,6},{10,8},{12,10},{14,12},{16,14},{18,16},{20... | collective-permute-start | bytes 1966088 | tf_op jit(solution)/shard_map/ppermute | solution.py:30
  84.7 15.4 %collective-permute-start.4 = (bf16[128,1,16,160]{0,3,2,1:T(8,128)(2,1)S(1)}, bf16[128,1,16,160]{0,3,2,1:T(8,128)(2,1)S(1)}, u32[]{:S(2)}, u32[]{:S(2)}) collective-permute-start(bf16[128,1,16,160]{0,3,2,1:T(8,128)(2,1)S(1)} %get-tuple-element.10), channel_id=1, source_target_pairs={{0,2},{2,4},{4,6},{6,8},{8,10},{10,12},{12,14},{14,16},{16,18},{18... | collective-permute-start | bytes 1966088 | tf_op jit(solution)/shard_map/ppermute | solution.py:27
  121.7 8.2 %collective-permute-start.7 = (bf16[128,1,16,160]{0,3,2,1:T(8,128)(2,1)S(1)}, bf16[128,1,16,160]{0,3,2,1:T(8,128)(2,1)S(1)}, u32[]{:S(2)}, u32[]{:S(2)}) collective-permute-start(bf16[128,1,16,160]{0,3,2,1:T(8,128)(2,1)S(1)} %get-tuple-element.9), channel_id=1, source_target_pairs={{2,0},{4,2},{6,4},{8,6},{10,8},{12,10},{14,12},{16,14},{18,16},{20... | collective-permute-start | bytes 1966088 | tf_op jit(solution)/shard_map/ppermute | solution.py:30
  121.8 14.2 %collective-permute-start.6 = (bf16[128,1,16,160]{0,3,2,1:T(8,128)(2,1)S(1)}, bf16[128,1,16,160]{0,3,2,1:T(8,128)(2,1)S(1)}, u32[]{:S(2)}, u32[]{:S(2)}) collective-permute-start(bf16[128,1,16,160]{0,3,2,1:T(8,128)(2,1)S(1)} %get-tuple-element.8), channel_id=1, source_target_pairs={{0,2},{2,4},{4,6},{6,8},{8,10},{10,12},{12,14},{14,16},{16,18},{18... | collective-permute-start | bytes 1966088 | tf_op jit(solution)/shard_map/ppermute | solution.py:27
  158.5 29.1 %collective-permute-start.8 = (bf16[128,2,16,160]{0,3,2,1:T(8,128)(2,1)}, bf16[128,2,16,160]{0,3,2,1:T(8,128)(2,1)}, u32[]{:S(2)}, u32[]{:S(2)}) collective-permute-start(bf16[128,2,16,160]{0,3,2,1:T(8,128)(2,1)} %fusion.26), channel_id=1, source_target_pairs={{0,1},{1,0},{2,3},{3,2},{4,5},{5,4},{6,7},{7,6},{8,9},{9,8},{10,11... | collective-permute-start | bytes 3932168 | tf_op jit(solution)/shard_map/ppermute | solution.py:14
  161.4 8.2 %collective-permute-start.10 = (bf16[128,1,16,160]{0,3,2,1:T(8,128)(2,1)S(1)}, bf16[128,1,16,160]{0,3,2,1:T(8,128)(2,1)S(1)}, u32[]{:S(2)}, u32[]{:S(2)}) collective-permute-start(bf16[128,1,16,160]{0,3,2,1:T(8,128)(2,1)S(1)} %get-tuple-element.7), channel_id=1, source_target_pairs={{2,0},{4,2},{6,4},{8,6},{10,8},{12,10},{14,12},{16,14},{18,16},{20... | collective-permute-start | bytes 1966088 | tf_op jit(solution)/shard_map/ppermute | solution.py:30
  161.5 15.0 %collective-permute-start.9 = (bf16[128,1,16,160]{0,3,2,1:T(8,128)(2,1)S(1)}, bf16[128,1,16,160]{0,3,2,1:T(8,128)(2,1)}, u32[]{:S(2)}, u32[]{:S(2)}) collective-permute-start(bf16[128,1,16,160]{0,3,2,1:T(8,128)(2,1)S(1)} %get-tuple-element.6), channel_id=1, source_target_pairs={{0,2},{2,4},{4,6},{6,8},{8,10},{10,12},{12,14},{14,16},{16,18},{18... | collective-permute-start | bytes 1966088 | tf_op jit(solution)/shard_map/ppermute | solution.py:27
Sparse Core Ops, SparseCore 0:
  206.0 59.8 reduce-scatter.1
